TPU v7x, 32 devices: a whole 2x2x4 slice. The times are simulated.
32 devices in a mesh: grp: 4 (over z), dev: 8 (over y, x, core).
Axes of the slice: x: 2, y: 2, z: 4, core: 2. Of those that a mesh axis runs over, the one named last changes fastest.
Arguments:
- sources: bfloat16 [8, 131072], P(None, ('grp', 'dev')), may hold values from -6 to 6
- boundary_impedance_input: float32 [8, 256], replicated, may hold values from -6 to 6
- leaf_inverse: bfloat16 [131072, 2048], P(('grp', 'dev')), may hold values from -0.1875 to 0.1875
- leaf_flux: bfloat16 [131072, 256], P(('grp', 'dev')), may hold values from -0.1875 to 0.1875
- leaf_lift: bfloat16 [16384, 2048], P(('grp', 'dev')), may hold values from -0.375 to 0.375
- node_schur: float32 [128, 64, 128], P(('grp', 'dev')), may hold values from -0.375 to 0.375
- node_spread: float32 [128, 64, 256], P(('grp', 'dev')), may hold values from -0.1875 to 0.1875
- node_lift: float32 [128, 128, 128], P(('grp', 'dev')), may hold values from -0.25 to 0.25
Outputs:
- field: float32 [8, 262144], P(None, ('grp', 'dev'))
All inputs are finite; a program needn't handle non-finite values.
Results may differ from a plain program's by a relative error of at most 0.0025.
Values sent between devices are 32-bit elements; how exact they have to be, the bound alone decides.
A program may use at most 128 MiB of HBM per device.

v0:
```python
import jax
import jax.numpy as jnp
from jax import lax
from jax.sharding import PartitionSpec as P


def complex_mul(vector, matrix):
    inner = matrix.shape[1]
    cols = matrix.shape[2] // 2
    hp = lax.Precision.HIGHEST
    from_real = jnp.einsum("nsa,nab->nsb", vector[..., :inner], matrix, precision=hp)
    from_imag = jnp.einsum("nsa,nab->nsb", vector[..., inner:], matrix, precision=hp)
    return jnp.concatenate(
        [
            from_real[..., :cols] - from_imag[..., cols:],
            from_real[..., cols:] + from_imag[..., :cols],
        ],
        -1,
    )


def select_component(vector, start, stop):
    half = vector.shape[-1] // 2
    return jnp.concatenate([vector[..., start:stop], vector[..., half + start : half + stop]], -1)


def join_parts(first, second):
    half_one = first.shape[-1] // 2
    half_two = second.shape[-1] // 2
    return jnp.concatenate(
        [
            first[..., :half_one],
            second[..., :half_two],
            first[..., half_one:],
            second[..., half_two:],
        ],
        -1,
    )


def merge_pair(left_out, right_out, schur, spread):
    width = left_out.shape[-1] // 4
    jump = complex_mul(
        select_component(right_out, width, 2 * width)
        - select_component(left_out, width, 2 * width),
        schur,
    )
    parent = join_parts(
        select_component(left_out, 0, width), select_component(right_out, 0, width)
    ) + complex_mul(jump, spread)
    return (jump, parent)


def split_children(incoming, iface):
    width = incoming.shape[-1] // 4
    return (
        join_parts(select_component(incoming, 0, width), iface),
        join_parts(select_component(incoming, width, 2 * width), iface),
    )


def ascend(outgoing, schur, spread):
    levels = outgoing.shape[0].bit_length() - 1
    jumps = []
    for tier_index in range(levels):
        half_step = 2**tier_index
        jump, outgoing = merge_pair(
            outgoing[0::2],
            outgoing[1::2],
            schur[half_step :: 2 * half_step],
            spread[half_step :: 2 * half_step],
        )
        jumps.append(jump)
    return (outgoing, jumps)


def descend(incoming, jumps, lift):
    for tier_index in reversed(range(len(jumps))):
        half_step = 2**tier_index
        iface = complex_mul(incoming, lift[half_step :: 2 * half_step]) + jumps[tier_index]
        left_in, right_in = split_children(incoming, iface)
        incoming = jnp.stack([left_in, right_in], 1).reshape(
            -1, incoming.shape[1], incoming.shape[2]
        )
    return incoming


def body(
    sources,
    boundary_impedance_input,
    leaf_inverse,
    leaf_flux,
    leaf_lift,
    node_schur,
    node_spread,
    node_lift,
):
    source_count = sources.shape[0]
    leaves_here = node_schur.shape[0]
    cell_count = leaf_inverse.shape[1] // 2
    interface_edge_count = leaf_flux.shape[1] // 2
    source_blocks = sources.reshape(source_count, leaves_here, cell_count)
    leaf_out = jnp.einsum(
        "slc,lce->lse",
        source_blocks,
        leaf_flux.reshape(leaves_here, cell_count, 2 * interface_edge_count),
        preferred_element_type=jnp.float32,
    )
    local_root, local_jumps = ascend(leaf_out, node_schur, node_spread)
    place = lax.axis_index("grp") * lax.axis_size("dev") + lax.axis_index("dev")
    roots = lax.all_gather(local_root, ("grp", "dev"), axis=0, tiled=True)
    schur_all, spread_all, lift_all = (
        lax.all_gather(node_schur[0:1], ("grp", "dev"), axis=0, tiled=True),
        lax.all_gather(node_spread[0:1], ("grp", "dev"), axis=0, tiled=True),
        lax.all_gather(node_lift[0:1], ("grp", "dev"), axis=0, tiled=True),
    )
    top_out, tree_jumps = ascend(roots, schur_all, spread_all)
    incoming_all = descend(boundary_impedance_input[None], tree_jumps, lift_all)
    device_in = lax.dynamic_slice_in_dim(incoming_all, place, 1, 0)
    incoming = descend(device_in, local_jumps, node_lift)
    leaf_input_values = incoming.astype(jnp.bfloat16)
    particular = jnp.einsum(
        "vfz,fzo->vfo",
        source_blocks,
        leaf_inverse.reshape(leaves_here, cell_count, 2 * cell_count),
        preferred_element_type=jnp.float32,
    )
    lifting_operator = leaf_lift.reshape(leaves_here, interface_edge_count, 2 * cell_count)
    from_real = jnp.einsum(
        "kpi,kih->pkh",
        leaf_input_values[..., :interface_edge_count],
        lifting_operator,
        preferred_element_type=jnp.float32,
    )
    from_imag = jnp.einsum(
        "kpi,kih->pkh",
        leaf_input_values[..., interface_edge_count:],
        lifting_operator,
        preferred_element_type=jnp.float32,
    )
    lifted = jnp.concatenate(
        [
            from_real[..., :cell_count] - from_imag[..., cell_count:],
            from_real[..., cell_count:] + from_imag[..., :cell_count],
        ],
        -1,
    )
    field = particular + lifted
    return field.reshape(source_count, leaves_here * 2 * cell_count)


def solution(mesh):
    in_specs = (
        P(None, ("grp", "dev")),
        P(),
        P(("grp", "dev"), None),
        P(("grp", "dev"), None),
        P(("grp", "dev"), None),
        P(("grp", "dev"), None, None),
        P(("grp", "dev"), None, None),
        P(("grp", "dev"), None, None),
    )
    out_specs = P(None, ("grp", "dev"))
    return jax.shard_map(body, mesh=mesh, in_specs=in_specs, out_specs=out_specs, check_vma=False)
```

profile of v0, /device:TPU:0, one launch (start us, length us, event | category | flops | bytes accessed | tf_op | source)
XLA Modules:
  0.0 212.5 jit_solution(15684005119780731152)
XLA Ops:
  6.5 1.5 slice.828
  8.1 1.5 slice.833
  9.7 1.5 slice.768
  11.2 2.0 fusion.166
  13.3 0.2 fusion.77
  13.6 0.2 fusion.79
  13.8 0.2 fusion.53
  14.0 0.2 fusion.55
  14.6 0.2 convolution_bitcast_fusion.9
  15.3 44.0 %all_gather.13 = f32[32,8,256]{2,1,0:T(8,128)S(1)} all-gather(f32[1,8,256]{2,1,0:T(8,128)S(1)} %maximum_add_fusion.8), channel_id=1, replica_groups=mesh['grp'=4,'dev'=8] {'grp','dev'}, dimensions={0}, use_global_device_ids=true | all-gather | bytes 270336 | tf_op jit(solution)/shard_map/all_gather | solution.py:111
  59.7 7.2 %all-gather.6.cloned.1.call-done = f32[32,64,128]{2,1,0:T(8,128)} async-done(((f32[1,64,128]{2,1,0:T(8,128)}), f32[32,64,128]{2,1,0:T(8,128)}) %all-gather.6.cloned.1.call-update) | async-done | bytes 1048592 | tf_op jit(solution)/shard_map/all_gather | solution.py:113
  66.9 1.6 fusion.19
  68.5 1.6 fusion.17
  70.2 54.9 %all-gather.8.cloned.1.call-done = f32[32,64,256]{2,1,0:T(8,128)} async-done(((f32[1,64,256]{2,1,0:T(8,128)}), f32[32,64,256]{2,1,0:T(8,128)}) %all-gather.8.cloned.1.call-update) | async-done | bytes 2097168 | tf_op jit(solution)/shard_map/all_gather | solution.py:114
  125.1 1.9 fusion.5
  127.0 2.0 fusion.7
  129.5 0.3 fusion.31
  129.8 0.4 fusion.29
  130.3 0.4 fusion.15
  130.7 0.4 fusion.13
  131.4 0.2 fusion.51
  131.6 0.3 fusion.49
  132.0 0.2 fusion.27
  132.2 0.2 fusion.25
  132.8 0.2 fusion.73
  133.0 0.2 fusion.71
  133.3 0.2 fusion.47
  133.5 0.2 fusion.45
  134.0 0.2 convolution_bitcast_fusion.7
  134.3 48.9 %all-gather.4.cloned.1.call-done = f32[32,128,128]{2,1,0:T(8,128)} async-done(((f32[1,128,128]{2,1,0:T(8,128)}), f32[32,128,128]{2,1,0:T(8,128)}) %all-gather.4.cloned.1.call-update) | async-done | bytes 2097168 | tf_op jit(solution)/shard_map/all_gather | solution.py:115
  183.3 1.1 convolution_bitcast_fusion.11
  184.4 1.0 convolution_bitcast_fusion.12
  185.8 1.1 fusion.43
  186.9 1.1 fusion.41
  188.5 1.3 fusion.23
  189.8 1.3 fusion.21
  191.5 0.5 fusion.11
  192.0 0.5 fusion.9
  193.0 1.0 fusion.3
  194.0 1.0 fusion.1
  195.5 0.2 convolution_bitcast_fusion.6
  195.7 0.2 convolution_bitcast_fusion.5
  196.2 0.2 fusion.37
  196.5 0.2 fusion.39
  197.1 0.4 convolution_bitcast_fusion
  197.5 0.4 convolution_bitcast_fusion.1
  197.9 0.4 copy-done.7
  198.3 7.7 %fusion = f32[8,4,2048]{2,0,1:T(8,128)} fusion(bf16[4,1024,2048]{2,1,0:T(8,128)(2,1)} %bitcast.144, bf16[8,4,1024]{2,0,1:T(8,128)(2,1)S(1)} %bitcast.159, f32[8,4,1024]{2,0,1:T(8,128)S(1)} %get-tuple-element.6, f32[8,4,1024]{2,0,1:T(8,128)S(1)} %get-tuple-element.5), kind=kOutput, calls=%fused_computation.3 | convolution fusion | flops 134348800 | bytes 17367040 | tf_op jit(solution)/shard_map/vfz,fzo->vfo/dot_general | solution.py:122
  (118 shorter events, 6.5 us)
Async XLA Ops:
  6.5 190.6 %copy-start = (bf16[512,2048]{1,0:T(8,128)(2,1)S(1)}, bf16[512,2048]{1,0:T(8,128)(2,1)}, u32[]{:S(2)}) copy-start(bf16[512,2048]{1,0:T(8,128)(2,1)} %param.12) | copy-start | bytes 6291460
  6.5 6.8 %copy-start.6 = (f32[4,64,128]{2,1,0:T(8,128)S(1)}, f32[4,64,128]{2,1,0:T(8,128)}, u32[]{:S(2)}) copy-start(f32[4,64,128]{2,1,0:T(8,128)} %param.13) | copy-start | bytes 393220
  6.5 7.3 %copy-start.5 = (f32[4,64,256]{2,1,0:T(8,128)S(1)}, f32[4,64,256]{2,1,0:T(8,128)}, u32[]{:S(2)}) copy-start(f32[4,64,256]{2,1,0:T(8,128)} %param.14) | copy-start | bytes 786436
  6.5 60.3 %all-gather.6.cloned.1.call-start = ((), (), s32[]{:S(2)}) async-start(), calls=%async_computation.1 | async-start | bytes 1081344 | tf_op jit(solution)/shard_map/all_gather | solution.py:113
  8.1 117.0 %all-gather.8.cloned.1.call-start = ((), (), s32[]{:S(2)}) async-start(), calls=%async_computation.2 | async-start | bytes 2162688 | tf_op jit(solution)/shard_map/all_gather | solution.py:114
  9.6 173.6 %all-gather.4.cloned.1.call-start = ((), (), s32[]{:S(2)}) async-start(), calls=%async_computation | async-start | bytes 2162688 | tf_op jit(solution)/shard_map/all_gather | solution.py:115
  13.2 46.3 %copy-start.8 = (f32[8,256]{1,0:T(8,128)S(1)}, f32[8,256]{1,0:T(8,128)}, u32[]{:S(2)}) copy-start(f32[8,256]{1,0:T(8,128)} %param.9) | copy-start | bytes 24580
  125.1 4.4 %copy-start.3 = (f32[32,64,128]{2,1,0:T(8,128)S(1)}, f32[32,64,128]{2,1,0:T(8,128)}, u32[]{:S(2)}) copy-start(f32[32,64,128]{2,1,0:T(8,128)} %all-gather.6.cloned.1.call-done) | copy-start | bytes 3145732
  127.0 3.2 %copy-start.2 = (f32[32,64,256]{2,1,0:T(8,128)S(1)}, f32[32,64,256]{2,1,0:T(8,128)}, u32[]{:S(2)}) copy-start(f32[32,64,256]{2,1,0:T(8,128)} %all-gather.8.cloned.1.call-done) | copy-start | bytes 6291460
  183.3 8.2 %copy-start.1 = (f32[32,128,128]{2,1,0:T(8,128)S(1)}, f32[32,128,128]{2,1,0:T(8,128)}, u32[]{:S(2)}) copy-start(f32[32,128,128]{2,1,0:T(8,128)} %all-gather.4.cloned.1.call-done) | copy-start | bytes 6291460
  194.0 1.5 copy-start.4
  197.5 0.8 copy-start.7
Sparse Core Ops, SparseCore 0:
  10.2 56.6 all-gather.5
  69.7 55.3 all-gather.7
  128.0 55.2 all-gather.3
where the time goes:
time: 213 us
  waiting for transfers between devices  111 us (52%)
  blocking collectives  44 us (21%)
  matrix products  33.3 us (16%)
  between operations  13.4 us (6%)
  local copies, waits for them, and re-layouts  6.94 us (3%)
  other arithmetic  3.7 us (2%)
    all_gather x1, waiting for transfers between devices, body(): lax.all_gather(node_spread[0:1], ('grp', 'dev'), axis=0, tiled=True)  54.9 us
    all_gather x1, waiting for transfers between devices, body(): lax.all_gather(node_lift[0:1], ('grp', 'dev'), axis=0, tiled=True)  48.9 us
    all_gather x1, blocking collectives, body(): roots = lax.all_gather(local_root, ('grp', 'dev'), axis=0, tiled=True)  44 us
    dot_general x20, matrix products, complex_mul(): jnp.einsum('nsa,nab->nsb', vector[..., inner:], matrix, precision=hp)  11.7 us
    dot_general x20, matrix products, complex_mul(): jnp.einsum('nsa,nab->nsb', vector[..., :inner], matrix, precision=hp)  11.1 us
    dot_general x1, matrix products, body(): jnp.einsum('vfz,fzo->vfo', source_blocks, leaf_inverse.reshape(leaves_her...  7.68 us
    all_gather x1, waiting for transfers between devices, body(): lax.all_gather(node_schur[0:1], ('grp', 'dev'), axis=0, tiled=True)  7.18 us
  transfers between devices with their start and end apart: 3, of which 3 were waited for; matrix products, arithmetic and copies ran while one was open for 9% of the time, Pallas kernels for 0%

commit v1 on v0

v1 whole, which is shorter than its diff:
```python
import functools

import jax
import jax.numpy as jnp
from jax import lax
from jax.experimental import pallas as pl
from jax.experimental.pallas import tpu as pltpu
from jax.sharding import PartitionSpec as P

MESH = pl.DeviceIdType.MESH
BF16 = jnp.bfloat16
F32 = jnp.float32


def dot(a, b):
    return jnp.dot(a, b, preferred_element_type=F32)


def split(x):
    hi = x.astype(BF16)
    return hi, (x - hi.astype(F32)).astype(BF16)


def combine(r, n):
    s = r.shape[0] // 2
    return jnp.concatenate([r[:s, :n] - r[s:, n:], r[s:, :n] + r[:s, n:]], 0)


def cmul(v, w):
    v_hi, v_lo = split(v)
    w_hi, w_lo = split(w)
    rows = v.shape[0]
    both = dot(jnp.concatenate([v_hi, v_lo], 0), w_hi)
    return combine(both[:rows] + both[rows:] + dot(v_hi, w_lo), w.shape[1] // 2)


def fold(x):
    n = x.shape[1] // 2
    return jnp.concatenate([x[:, :n], x[:, n:]], 0)


def join(a, b):
    return jnp.concatenate([a, b], 1)


def kernel(
    ng,
    nd,
    nl,
    src_ref,
    bnd_ref,
    inv_hbm,
    flux_hbm,
    ll_hbm,
    schur_hbm,
    spread_hbm,
    lift_hbm,
    out_ref,
    inv,
    flux,
    ll,
    fac_loc,
    fac_all,
    top,
    roots,
    groots,
    jump_loc,
    jump_all,
    jump_top,
    inv_sem,
    flux_sem,
    ll_sem,
    fl_sem,
    fa_sem,
    top_sem,
    fs_sem,
    fr_sem,
    bs_sem,
    br_sem,
    rs_sem,
    rr_sem,
    zs_sem,
    zr_sem,
    ws_sem,
    wr_sem,
    gs_sem,
    gr_sem,
):
    grp = lax.axis_index("grp")
    dev = lax.axis_index("dev")
    nc = nd // 2
    core = lax.rem(dev, 2)
    chip = dev // 2
    sib = chip * 2 + (1 - core)
    iface = schur_hbm.shape[1]
    edge = lift_hbm.shape[1]
    cells = inv.shape[0] // nl
    frows = fac_all.shape[1]
    half = frows // 2
    o_sp, o_im, o_li = iface, 2 * iface, 3 * iface

    flux_cp = [
        pltpu.make_async_copy(
            flux_hbm.at[pl.ds(l * cells, cells)], flux.at[pl.ds(l * cells, cells)], flux_sem.at[l]
        )
        for l in range(nl)
    ]
    def factor_copies(pick, dst, sems):
        parts = (
            (schur_hbm.at[pick], 0, iface),
            (spread_hbm.at[pick, :, pl.ds(0, edge)], o_sp, iface),
            (spread_hbm.at[pick, :, pl.ds(edge, edge)], o_im, iface),
            (lift_hbm.at[pick], o_li, edge),
        )
        return [
            pltpu.make_async_copy(ref, dst.at[pl.ds(off, rows)], sems.at[i])
            for i, (ref, off, rows) in enumerate(parts)
        ]

    fa_cp = factor_copies(0, fac_all.at[dev], fa_sem)
    fl_cp = [factor_copies(l, fac_loc.at[l], fl_sem.at[l]) for l in range(1, nl)]
    for cp in fa_cp + flux_cp:
        cp.start()
    for cps in fl_cp:
        for cp in cps:
            cp.start()

    barrier = pltpu.get_barrier_semaphore()
    for k in range(1, nd):
        pl.semaphore_signal(
            barrier, inc=1, device_id=(grp, lax.rem(dev + k, nd)), device_id_type=MESH
        )
    for k in range(1, ng):
        pl.semaphore_signal(
            barrier, inc=1, device_id=(lax.rem(grp + k, ng), dev), device_id_type=MESH
        )
    pl.semaphore_wait(barrier, nd - 1 + ng - 1)

    def remote(src, dst, ssem, rsem, g, d):
        return pltpu.make_async_remote_copy(
            src_ref=src, dst_ref=dst, send_sem=ssem, recv_sem=rsem,
            device_id=(g, d), device_id_type=MESH,
        )

    for cp in fa_cp:
        cp.wait()
    fac_send = [
        remote(
            fac_all.at[dev], fac_all.at[dev], fs_sem.at[k], fr_sem.at[k],
            grp, lax.rem(chip + k, nc) * 2 + core,
        )
        for k in range(1, nc)
    ]
    for cp in fac_send:
        cp.start()

    def pass_on(k):
        owner = lax.rem(chip + nc - k, nc) * 2 + core
        return remote(fac_all.at[owner], fac_all.at[owner], bs_sem.at[k], br_sem.at[k], grp, sib)

    fac_pass = [pass_on(k) for k in range(nc)]
    fac_pass[0].start()

    units = 2 * nl
    rows_u = cells // 2
    inv_cp = [
        pltpu.make_async_copy(
            inv_hbm.at[pl.ds(u * rows_u, rows_u)], inv.at[pl.ds(u * rows_u, rows_u)], inv_sem.at[u]
        )
        for u in range(units)
    ]
    ll_cp = pltpu.make_async_copy(ll_hbm, ll, ll_sem.at[0])

    for cp in flux_cp:
        cp.wait()
    for cp in inv_cp:
        cp.start()
    ll_cp.start()

    def merge(a, b, fac, jump_dst):
        diff = (b - a)[:, iface:]
        jump = cmul(diff, fac[0:iface, :])
        jump_dst[...] = jump
        spread = jnp.concatenate([fac[o_sp:o_im, :], fac[o_im:o_li, :]], 1)
        return join(a[:, :iface], b[:, :iface]) + cmul(jump, spread)

    def lower(inc, fac, jump):
        return cmul(inc, fac[o_li:frows, :]) + jump

    def climb(outs, fac_of, jump_of):
        half_step = 1
        while len(outs) > 1:
            outs = [
                merge(
                    outs[2 * i],
                    outs[2 * i + 1],
                    fac_of((2 * i + 1) * half_step),
                    jump_of((2 * i + 1) * half_step),
                )
                for i in range(len(outs) // 2)
            ]
            half_step *= 2
        return outs[0]

    outs = [
        fold(dot(src_ref[:, l * cells : (l + 1) * cells], flux[l * cells : (l + 1) * cells, :]))
        for l in range(nl)
    ]
    for cps in fl_cp:
        for cp in cps:
            cp.wait()
    roots[dev] = climb(outs, lambda s: fac_loc.at[s], lambda s: jump_loc.at[s])
    root_send = [
        remote(
            roots.at[dev], roots.at[dev], rs_sem.at[k], rr_sem.at[k], grp, lax.rem(dev + k, nd)
        )
        for k in range(1, nd)
    ]
    for cp in root_send:
        cp.start()

    width = 2 * cells

    def unit(u):
        inv_cp[u].wait()
        l = u // 2
        part = dot(
            src_ref[:, u * rows_u : (u + 1) * rows_u], inv[u * rows_u : (u + 1) * rows_u, :]
        )
        cols = slice(l * width, (l + 1) * width)
        if u % 2 == 0:
            out_ref[:, cols] = part
        else:
            out_ref[:, cols] += part

    def run_units(lo, hi):
        for u in range(lo, hi):
            unit(u)

    cut = [units * i // 8 for i in (0, 2, 3, 5, 8)]
    run_units(cut[0], cut[1])
    for k in range(1, nc):
        fac_send[k - 1].wait_recv()
        fac_pass[k].start()
    run_units(cut[1], cut[2])
    for cp in fac_pass:
        cp.wait_recv()
    rows_mine = pl.ds(pl.multiple_of(core * half, 8), half)
    top_own = pltpu.make_async_copy(fac_all.at[0], top.at[grp], top_sem.at[0])
    top_own.start()
    top_send = [
        remote(
            fac_all.at[0, rows_mine], top.at[grp, rows_mine], zs_sem.at[k], zr_sem.at[k],
            lax.rem(grp + k, ng), dev,
        )
        for k in range(1, ng)
    ]
    for cp in top_send:
        cp.start()

    for cp in root_send:
        cp.wait_recv()
    groots[grp] = climb(
        [roots[d] for d in range(nd)], lambda s: fac_all.at[s], lambda s: jump_all.at[s]
    )
    groot_send = [
        remote(
            groots.at[grp], groots.at[grp], gs_sem.at[k], gr_sem.at[k], lax.rem(grp + k, ng), dev
        )
        for k in range(1, ng)
    ]
    for cp in groot_send:
        cp.start()
    run_units(cut[2], cut[3])

    top_pass = []
    for k in range(1, ng):
        owner = lax.rem(grp + ng - k, ng)
        top_send[k - 1].wait_recv()
        cp = remote(
            top.at[owner, rows_mine], top.at[owner, rows_mine], ws_sem.at[k], wr_sem.at[k], grp, sib
        )
        cp.start()
        top_pass.append(cp)
    run_units(cut[3], cut[4])
    for cp in groot_send:
        cp.wait_recv()
    top_own.wait()
    for cp in top_pass:
        cp.wait_recv()
    climb([groots[g] for g in range(ng)], lambda s: top.at[s], lambda s: jump_top.at[s])

    inc = fold(bnd_ref[...])

    def follow(inc, place, count, fac, jumps):
        step = count // 2
        while step >= 1:
            s = (place // (2 * step)) * (2 * step) + step
            low = lower(inc, fac.at[s], jumps[s])
            right = lax.rem(place // step, 2) == 1
            inc = join(jnp.where(right, inc[:, iface:], inc[:, :iface]), low)
            step //= 2
        return inc

    inc = follow(inc, grp, ng, top, jump_top)
    inc = follow(inc, dev, nd, fac_all, jump_all)
    incs = [inc]
    step = nl // 2
    while step >= 1:
        below = []
        for i, inc in enumerate(incs):
            s = (2 * i + 1) * step
            low = lower(inc, fac_loc.at[s], jump_loc[s])
            below.append(join(inc[:, :iface], low))
            below.append(join(inc[:, iface:], low))
        incs = below
        step //= 2

    ll_cp.wait()
    for l in range(nl):
        lifted = dot(incs[l].astype(BF16), ll[l * edge : (l + 1) * edge, :])
        s = lifted.shape[0] // 2
        re = slice(l * width, l * width + cells)
        im = slice(l * width + cells, (l + 1) * width)
        out_ref[:, re] += lifted[:s, :cells] - lifted[s:, cells:]
        out_ref[:, im] += lifted[:s, cells:] + lifted[s:, :cells]

    for cp in fac_send + fac_pass + root_send + top_send + top_pass + groot_send:
        cp.wait_send()


def body(ng, nd, sources, boundary, inverse, flux, leaf_lift, schur, spread, lift):
    nl, iface = schur.shape[:2]
    edge = lift.shape[1]
    s = sources.shape[0]
    frows = 3 * iface + edge
    dma = pltpu.SemaphoreType.DMA
    nc = nd // 2
    vmem = pl.BlockSpec(memory_space=pltpu.VMEM)
    hbm = pl.BlockSpec(memory_space=pl.ANY)
    return pl.pallas_call(
        functools.partial(kernel, ng, nd, nl),
        out_shape=jax.ShapeDtypeStruct((s, nl * inverse.shape[1]), F32),
        in_specs=[vmem, vmem] + [hbm] * 6,
        out_specs=vmem,
        scratch_shapes=[
            pltpu.VMEM(inverse.shape, BF16),
            pltpu.VMEM(flux.shape, BF16),
            pltpu.VMEM(leaf_lift.shape, BF16),
            pltpu.VMEM((nl, frows, edge), F32),
            pltpu.VMEM((nd, frows, edge), F32),
            pltpu.VMEM((ng, frows, edge), F32),
            pltpu.VMEM((nd, 2 * s, edge), F32),
            pltpu.VMEM((ng, 2 * s, edge), F32),
            pltpu.VMEM((nl, 2 * s, iface), F32),
            pltpu.VMEM((nd, 2 * s, iface), F32),
            pltpu.VMEM((ng, 2 * s, iface), F32),
            dma((2 * nl,)),
            dma((nl,)),
            dma((1,)),
            dma((nl, 4)),
            dma((4,)),
            dma((1,)),
            dma((nc,)),
            dma((nc,)),
            dma((nc,)),
            dma((nc,)),
            dma((nd,)),
            dma((nd,)),
            dma((ng,)),
            dma((ng,)),
            dma((ng,)),
            dma((ng,)),
            dma((ng,)),
            dma((ng,)),
        ],
        compiler_params=pltpu.CompilerParams(
            collective_id=0, has_side_effects=True, vmem_limit_bytes=48 * 1024 * 1024
        ),
    )(sources, boundary, inverse, flux, leaf_lift, schur, spread, lift)


def solution(mesh):
    ng, nd = mesh.shape["grp"], mesh.shape["dev"]
    split_rows = P(("grp", "dev"), None)
    split_nodes = P(("grp", "dev"), None, None)
    in_specs = (
        P(None, ("grp", "dev")),
        P(),
        split_rows,
        split_rows,
        split_rows,
        split_nodes,
        split_nodes,
        split_nodes,
    )
    return jax.shard_map(
        functools.partial(body, ng, nd),
        mesh=mesh,
        in_specs=in_specs,
        out_specs=P(None, ("grp", "dev")),
        check_vma=False,
    )
```

time: 213 us -> 37.7 us (0.18)
  waiting for transfers between devices: 111 us -> 0 us
  blocking collectives: 44 us -> 0 us
  matrix products: 33.3 us -> 0 us
  Pallas kernels: 0 us -> 29.2 us
  between operations: 13.4 us -> 0.02 us
  other arithmetic: 3.7 us -> 0 us
    all_gather x3 -> x0, waiting for transfers between devices: 111 us -> none  [the longest x1 54.9 us: body(): lax.all_gather(node_spread[0:1], ('grp', 'dev'), axis=0, tiled=True)]
    all_gather x1 -> x0, blocking collectives: 44 us -> none  [body(): roots = lax.all_gather(local_root, ('grp', 'dev'), axis=0, tiled=True)]
    dot_general x44 -> x0, matrix products: 33.3 us -> none  [the longest x20 11.7 us: complex_mul(): jnp.einsum('nsa,nab->nsb', vector[..., inner:], matrix, precision=hp)]
    pallas_call x0 -> x1, Pallas kernels: none -> 29.2 us  [body(): pl.pallas_call(functools.partial(kernel, ng, nd, nl), out_shape=jax.Shape...]
    unnamed x18 -> x15, local copies, waits for them, and re-layouts: 0.45 us -> 8.22 us
    slice x33 -> x0, local copies, waits for them, and re-layouts: 6.45 us -> none  [the longest x1 1.51 us: body(): node_schur[0:1]]
  transfers between devices with their start and end apart: 3 -> 0, of which waited for: 3 -> 0; matrix products, arithmetic and copies ran while one was open for 9% -> 0% of each run, Pallas kernels for 0% -> 0%
where the time goes in v1:
time: 37.7 us; the launch traced here: 37.4 us
  Pallas kernels  29.2 us (77%)
  local copies, waits for them, and re-layouts  8.22 us (22%)
    pallas_call x1, Pallas kernels, body(): pl.pallas_call(functools.partial(kernel, ng, nd, nl), out_shape=jax.Shape...  29.2 us
    unnamed x15, local copies, waits for them, and re-layouts  8.22 us

profile of v1, /device:TPU:0, one launch (start us, length us, event | category | flops | bytes accessed | tf_op | source)
XLA Modules:
  0.0 37.4 jit_solution(1613814080056590007)
XLA Ops:
  0.0 0.0 copy-start
  0.0 1.6 %copy-done = bf16[4096,256]{1,0:T(8,128)(2,1)S(1)} copy-done((bf16[4096,256]{1,0:T(8,128)(2,1)S(1)}, bf16[4096,256]{1,0:T(8,128)(2,1)}, u32[]{:S(2)}) %copy-start) | copy-done | bytes 2097176
  1.6 0.0 copy-start.1
  1.6 1.6 %copy-done.1 = bf16[512,2048]{1,0:T(8,128)(2,1)S(1)} copy-done((bf16[512,2048]{1,0:T(8,128)(2,1)S(1)}, bf16[512,2048]{1,0:T(8,128)(2,1)}, u32[]{:S(2)}) %copy-start.1) | copy-done | bytes 2097176
  3.2 0.0 copy-start.2
  3.2 0.9 %copy-done.2 = f32[4,64,256]{2,1,0:T(8,128)S(1)} copy-done((f32[4,64,256]{2,1,0:T(8,128)S(1)}, f32[4,64,256]{2,1,0:T(8,128)}, u32[]{:S(2)}) %copy-start.2) | copy-done | bytes 262168
  4.1 0.0 copy-start.3
  4.1 0.9 %copy-done.3 = f32[4,128,128]{2,1,0:T(8,128)S(1)} copy-done((f32[4,128,128]{2,1,0:T(8,128)S(1)}, f32[4,128,128]{2,1,0:T(8,128)}, u32[]{:S(2)}) %copy-start.3) | copy-done | bytes 262168
  5.1 0.0 copy-start.4
  5.1 0.9 %copy-done.4 = f32[4,64,128]{2,1,0:T(8,128)S(1)} copy-done((f32[4,64,128]{2,1,0:T(8,128)S(1)}, f32[4,64,128]{2,1,0:T(8,128)}, u32[]{:S(2)}) %copy-start.4) | copy-done | bytes 131096
  6.0 0.0 copy-start.5
  6.0 0.8 %copy-done.5 = bf16[8,4096]{1,0:T(8,128)(2,1)S(1)} copy-done((bf16[8,4096]{1,0:T(8,128)(2,1)S(1)}, bf16[8,4096]{1,0:T(8,128)(2,1)}, u32[]{:S(2)}) %copy-start.5) | copy-done | bytes 65560
  6.8 0.0 copy-start.6
  6.8 0.7 %copy-done.6 = f32[8,256]{1,0:T(8,128)S(1)} copy-done((f32[8,256]{1,0:T(8,128)S(1)}, f32[8,256]{1,0:T(8,128)}, u32[]{:S(2)}) %copy-start.6) | copy-done | bytes 8216
  7.5 29.2 %shard_map.82 = f32[8,8192]{1,0:T(8,128)S(1)} custom-call(bf16[8,4096]{1,0:T(8,128)(2,1)S(1)} %copy-done.5, f32[8,256]{1,0:T(8,128)S(1)} %copy-done.6, bf16[4096,2048]{1,0:T(8,128)(2,1)} %inv_hbm.1, bf16[4096,256]{1,0:T(8,128)(2,1)S(1)} %copy-done, bf16[512,2048]{1,0:T(8,128)(2,1)S(1)} %copy-done.1, f32[4,64,128]{2,1,0:T(8,128)S(1)} %copy-done.4, ...), custom_call_target="tpu_custom_call" | custom-call | tf_op jit(solution)/shard_map/pallas_call | solution.py:341
  36.7 0.7 %copy.10 = f32[8,8192]{1,0:T(8,128)} copy(f32[8,8192]{1,0:T(8,128)S(1)} %shard_map.82) | data formatting | bytes 524288
Async XLA Ops:
  0.0 1.6 %copy-start = (bf16[4096,256]{1,0:T(8,128)(2,1)S(1)}, bf16[4096,256]{1,0:T(8,128)(2,1)}, u32[]{:S(2)}) copy-start(bf16[4096,256]{1,0:T(8,128)(2,1)} %flux_hbm.1) | copy-start | bytes 6291460
  1.6 1.6 %copy-start.1 = (bf16[512,2048]{1,0:T(8,128)(2,1)S(1)}, bf16[512,2048]{1,0:T(8,128)(2,1)}, u32[]{:S(2)}) copy-start(bf16[512,2048]{1,0:T(8,128)(2,1)} %ll_hbm.1) | copy-start | bytes 6291460
  3.2 0.9 %copy-start.2 = (f32[4,64,256]{2,1,0:T(8,128)S(1)}, f32[4,64,256]{2,1,0:T(8,128)}, u32[]{:S(2)}) copy-start(f32[4,64,256]{2,1,0:T(8,128)} %spread_hbm.1) | copy-start | bytes 786436
  4.1 0.9 %copy-start.3 = (f32[4,128,128]{2,1,0:T(8,128)S(1)}, f32[4,128,128]{2,1,0:T(8,128)}, u32[]{:S(2)}) copy-start(f32[4,128,128]{2,1,0:T(8,128)} %lift_hbm.1) | copy-start | bytes 786436
  5.1 0.9 %copy-start.4 = (f32[4,64,128]{2,1,0:T(8,128)S(1)}, f32[4,64,128]{2,1,0:T(8,128)}, u32[]{:S(2)}) copy-start(f32[4,64,128]{2,1,0:T(8,128)} %schur_hbm.1) | copy-start | bytes 393220
  6.0 0.8 %copy-start.5 = (bf16[8,4096]{1,0:T(8,128)(2,1)S(1)}, bf16[8,4096]{1,0:T(8,128)(2,1)}, u32[]{:S(2)}) copy-start(bf16[8,4096]{1,0:T(8,128)(2,1)} %src_ref.1) | copy-start | bytes 196612
  6.8 0.7 %copy-start.6 = (f32[8,256]{1,0:T(8,128)S(1)}, f32[8,256]{1,0:T(8,128)}, u32[]{:S(2)}) copy-start(f32[8,256]{1,0:T(8,128)} %bnd_ref.1) | copy-start | bytes 24580

commit v2 on v1

--- a/solution.py
+++ b/solution.py
@@ -1,4 +1,5 @@
 import functools
+import math
 
 import jax
 import jax.numpy as jnp
@@ -47,8 +48,8 @@
     ng,
     nd,
     nl,
-    src_ref,
-    bnd_ref,
+    src_hbm,
+    bnd_hbm,
     inv_hbm,
     flux_hbm,
     ll_hbm,
@@ -56,12 +57,15 @@
     spread_hbm,
     lift_hbm,
     out_ref,
+    src_ref,
+    bnd_ref,
     inv,
     flux,
     ll,
     fac_loc,
     fac_all,
     top,
+    pair,
     roots,
     groots,
     jump_loc,
@@ -70,6 +74,7 @@
     inv_sem,
     flux_sem,
     ll_sem,
+    sb_sem,
     fl_sem,
     fa_sem,
     top_sem,
@@ -77,12 +82,15 @@
     fr_sem,
     bs_sem,
     br_sem,
+    zs_sem,
+    zr_sem,
+    hs_sem,
+    hr_sem,
+    ws_sem,
+    wr_sem,
+    ps_sem,
     rs_sem,
     rr_sem,
-    zs_sem,
-    zr_sem,
-    ws_sem,
-    wr_sem,
     gs_sem,
     gr_sem,
 ):
@@ -96,7 +104,8 @@
     edge = lift_hbm.shape[1]
     cells = inv.shape[0] // nl
     frows = fac_all.shape[1]
-    half = frows // 2
+    npc = math.gcd(frows // 8, nc)
+    piece = frows // npc
     o_sp, o_im, o_li = iface, 2 * iface, 3 * iface
 
     flux_cp = [
@@ -119,12 +128,15 @@
 
     fa_cp = factor_copies(0, fac_all.at[dev], fa_sem)
     fl_cp = [factor_copies(l, fac_loc.at[l], fl_sem.at[l]) for l in range(1, nl)]
-    for cp in fa_cp + flux_cp:
+    src_cp = pltpu.make_async_copy(src_hbm, src_ref, sb_sem.at[0])
+    bnd_cp = pltpu.make_async_copy(bnd_hbm, bnd_ref, sb_sem.at[1])
+    for cp in fa_cp + [src_cp] + flux_cp + [bnd_cp]:
         cp.start()
     for cps in fl_cp:
         for cp in cps:
             cp.start()
 
+    relay = jnp.logical_and(core == 0, chip < npc)
     barrier = pltpu.get_barrier_semaphore()
     for k in range(1, nd):
         pl.semaphore_signal(
@@ -134,7 +146,21 @@
         pl.semaphore_signal(
             barrier, inc=1, device_id=(lax.rem(grp + k, ng), dev), device_id_type=MESH
         )
-    pl.semaphore_wait(barrier, nd - 1 + ng - 1)
+
+    @pl.when(jnp.logical_and(relay, chip > 0))
+    def _():
+        for k in range(1, ng):
+            pl.semaphore_signal(
+                barrier, inc=1, device_id=(lax.rem(grp + k, ng), 0), device_id_type=MESH
+            )
+
+    @pl.when(dev == 0)
+    def _():
+        pl.semaphore_wait(barrier, nd - 1 + (ng - 1) * npc)
+
+    @pl.when(dev != 0)
+    def _():
+        pl.semaphore_wait(barrier, nd - 1 + ng - 1)
 
     def remote(src, dst, ssem, rsem, g, d):
         return pltpu.make_async_remote_copy(
@@ -142,24 +168,67 @@
             device_id=(g, d), device_id_type=MESH,
         )
 
+    def same(ref, ssem, rsem, g, d):
+        return remote(ref, ref, ssem, rsem, g, d)
+
+    fac_send = [
+        same(
+            fac_all.at[dev], fs_sem.at[k], fr_sem.at[k], grp, lax.rem(chip + k, nc) * 2 + core
+        )
+        for k in range(1, nc)
+    ]
+    fac_pass = [
+        same(
+            fac_all.at[lax.rem(chip + nc - k, nc) * 2 + (core if k == 0 else 0)],
+            bs_sem.at[k], br_sem.at[k], grp, sib,
+        )
+        for k in range(nc)
+    ]
+    deal = [
+        remote(
+            fac_all.at[0, pl.ds(c * piece, piece)], top.at[grp, pl.ds(c * piece, piece)],
+            zs_sem.at[k, c], zr_sem.at[k], lax.rem(grp + k, ng), 2 * c,
+        )
+        for k in range(1, ng)
+        for c in range(npc)
+    ]
+    mine = pl.ds(pl.multiple_of(chip * piece, 8), piece)
+
+    def other(k):
+        return lax.rem(grp + ng - k, ng)
+
+    deal_in = [
+        same(top.at[other(k), mine], zs_sem.at[k, 0], zr_sem.at[k], grp, sib)
+        for k in range(1, ng)
+    ]
+    spread_out = [
+        [
+            same(
+                top.at[other(k), mine], hs_sem.at[k, j], hr_sem.at[k, j],
+                grp, lax.rem(chip + j, nc) * 2,
+            )
+            for j in range(1, nc)
+        ]
+        for k in range(1, ng)
+    ]
+    top_pass = [
+        same(top.at[other(k)], ws_sem.at[k], wr_sem.at[k], grp, sib) for k in range(1, ng)
+    ]
+
     for cp in fa_cp:
         cp.wait()
-    fac_send = [
-        remote(
-            fac_all.at[dev], fac_all.at[dev], fs_sem.at[k], fr_sem.at[k],
-            grp, lax.rem(chip + k, nc) * 2 + core,
-        )
-        for k in range(1, nc)
-    ]
-    for cp in fac_send:
-        cp.start()
-
-    def pass_on(k):
-        owner = lax.rem(chip + nc - k, nc) * 2 + core
-        return remote(fac_all.at[owner], fac_all.at[owner], bs_sem.at[k], br_sem.at[k], grp, sib)
-
-    fac_pass = [pass_on(k) for k in range(nc)]
+
     fac_pass[0].start()
+
+    @pl.when(core == 0)
+    def _():
+        for cp in fac_send:
+            cp.start()
+
+    @pl.when(dev == 0)
+    def _():
+        for cp in deal:
+            cp.start()
 
     units = 2 * nl
     rows_u = cells // 2
@@ -171,7 +240,7 @@
     ]
     ll_cp = pltpu.make_async_copy(ll_hbm, ll, ll_sem.at[0])
 
-    for cp in flux_cp:
+    for cp in [src_cp] + flux_cp:
         cp.wait()
     for cp in inv_cp:
         cp.start()
@@ -209,15 +278,9 @@
     for cps in fl_cp:
         for cp in cps:
             cp.wait()
-    roots[dev] = climb(outs, lambda s: fac_loc.at[s], lambda s: jump_loc.at[s])
-    root_send = [
-        remote(
-            roots.at[dev], roots.at[dev], rs_sem.at[k], rr_sem.at[k], grp, lax.rem(dev + k, nd)
-        )
-        for k in range(1, nd)
-    ]
-    for cp in root_send:
-        cp.start()
+    pair[core] = climb(outs, lambda s: fac_loc.at[s], lambda s: jump_loc.at[s])
+    pair_send = same(pair.at[core], ps_sem.at[0], ps_sem.at[1], grp, sib)
+    pair_send.start()
 
     width = 2 * cells
 
@@ -237,59 +300,82 @@
         for u in range(lo, hi):
             unit(u)
 
-    cut = [units * i // 8 for i in (0, 2, 3, 5, 8)]
+    cut = [units * i // 8 for i in (0, 2, 4, 6, 8)]
     run_units(cut[0], cut[1])
-    for k in range(1, nc):
-        fac_send[k - 1].wait_recv()
-        fac_pass[k].start()
+    fac_pass[0].wait_recv()
+    pair_send.wait_recv()
+    odd = chip * 2 + 1
+    roots[chip] = merge(pair[0], pair[1], fac_all.at[odd], jump_all.at[odd])
+    root_send = [
+        same(roots.at[chip], rs_sem.at[k], rr_sem.at[k], grp, lax.rem(chip + k, nc) * 2 + core)
+        for k in range(1, nc)
+    ]
+    for cp in root_send:
+        cp.start()
+
+    @pl.when(core == 0)
+    def _():
+        for k in range(1, nc):
+            fac_send[k - 1].wait_recv()
+            fac_pass[k].start()
+
+    @pl.when(relay)
+    def _():
+        for k in range(1, ng):
+            deal_in[k - 1].wait_recv()
+            for cp in spread_out[k - 1]:
+                cp.start()
+
     run_units(cut[1], cut[2])
-    for cp in fac_pass:
-        cp.wait_recv()
-    rows_mine = pl.ds(pl.multiple_of(core * half, 8), half)
+
+    @pl.when(core == 1)
+    def _():
+        for k in range(1, nc):
+            fac_pass[k].wait_recv()
+
     top_own = pltpu.make_async_copy(fac_all.at[0], top.at[grp], top_sem.at[0])
     top_own.start()
-    top_send = [
-        remote(
-            fac_all.at[0, rows_mine], top.at[grp, rows_mine], zs_sem.at[k], zr_sem.at[k],
-            lax.rem(grp + k, ng), dev,
-        )
-        for k in range(1, ng)
-    ]
-    for cp in top_send:
-        cp.start()
-
     for cp in root_send:
         cp.wait_recv()
     groots[grp] = climb(
-        [roots[d] for d in range(nd)], lambda s: fac_all.at[s], lambda s: jump_all.at[s]
+        [roots[c] for c in range(nc)], lambda s: fac_all.at[2 * s], lambda s: jump_all.at[2 * s]
     )
     groot_send = [
-        remote(
-            groots.at[grp], groots.at[grp], gs_sem.at[k], gr_sem.at[k], lax.rem(grp + k, ng), dev
-        )
+        same(groots.at[grp], gs_sem.at[k], gr_sem.at[k], lax.rem(grp + k, ng), dev)
         for k in range(1, ng)
     ]
     for cp in groot_send:
         cp.start()
     run_units(cut[2], cut[3])
 
-    top_pass = []
-    for k in range(1, ng):
-        owner = lax.rem(grp + ng - k, ng)
-        top_send[k - 1].wait_recv()
-        cp = remote(
-            top.at[owner, rows_mine], top.at[owner, rows_mine], ws_sem.at[k], wr_sem.at[k], grp, sib
-        )
-        cp.start()
-        top_pass.append(cp)
+    @pl.when(core == 0)
+    def _():
+        for k in range(1, ng):
+            for j in range(1, nc):
+                from_chip = lax.rem(chip + nc - j, nc)
+
+                def got(k=k, j=j):
+                    spread_out[k - 1][j - 1].wait_recv()
+
+                if npc == nc:
+                    got()
+                else:
+                    pl.when(from_chip < npc)(got)
+            top_pass[k - 1].start()
+
     run_units(cut[3], cut[4])
     for cp in groot_send:
         cp.wait_recv()
     top_own.wait()
-    for cp in top_pass:
-        cp.wait_recv()
+
+    @pl.when(core == 1)
+    def _():
+        for cp in top_pass:
+            cp.wait_recv()
+
     climb([groots[g] for g in range(ng)], lambda s: top.at[s], lambda s: jump_top.at[s])
 
+    bnd_cp.wait()
     inc = fold(bnd_ref[...])
 
     def follow(inc, place, count, fac, jumps):
@@ -325,8 +411,24 @@
         out_ref[:, re] += lifted[:s, :cells] - lifted[s:, cells:]
         out_ref[:, im] += lifted[:s, cells:] + lifted[s:, :cells]
 
-    for cp in fac_send + fac_pass + root_send + top_send + top_pass + groot_send:
+    for cp in [fac_pass[0], pair_send] + root_send + groot_send:
         cp.wait_send()
+
+    @pl.when(core == 0)
+    def _():
+        for cp in fac_send + fac_pass[1:] + top_pass:
+            cp.wait_send()
+
+    @pl.when(relay)
+    def _():
+        for cps in spread_out:
+            for cp in cps:
+                cp.wait_send()
+
+    @pl.when(dev == 0)
+    def _():
+        for cp in deal:
+            cp.wait_send()
 
 
 def body(ng, nd, sources, boundary, inverse, flux, leaf_lift, schur, spread, lift):
@@ -337,20 +439,23 @@
     dma = pltpu.SemaphoreType.DMA
     nc = nd // 2
     vmem = pl.BlockSpec(memory_space=pltpu.VMEM)
-    hbm = pl.BlockSpec(memory_space=pl.ANY)
+    hbm = pl.BlockSpec(memory_space=pltpu.MemorySpace.HBM)
     return pl.pallas_call(
         functools.partial(kernel, ng, nd, nl),
         out_shape=jax.ShapeDtypeStruct((s, nl * inverse.shape[1]), F32),
-        in_specs=[vmem, vmem] + [hbm] * 6,
+        in_specs=[hbm] * 8,
         out_specs=vmem,
         scratch_shapes=[
+            pltpu.VMEM(sources.shape, BF16),
+            pltpu.VMEM(boundary.shape, F32),
             pltpu.VMEM(inverse.shape, BF16),
             pltpu.VMEM(flux.shape, BF16),
             pltpu.VMEM(leaf_lift.shape, BF16),
             pltpu.VMEM((nl, frows, edge), F32),
             pltpu.VMEM((nd, frows, edge), F32),
             pltpu.VMEM((ng, frows, edge), F32),
-            pltpu.VMEM((nd, 2 * s, edge), F32),
+            pltpu.VMEM((2, 2 * s, edge), F32),
+            pltpu.VMEM((nc, 2 * s, edge), F32),
             pltpu.VMEM((ng, 2 * s, edge), F32),
             pltpu.VMEM((nl, 2 * s, iface), F32),
             pltpu.VMEM((nd, 2 * s, iface), F32),
@@ -358,6 +463,7 @@
             dma((2 * nl,)),
             dma((nl,)),
             dma((1,)),
+            dma((2,)),
             dma((nl, 4)),
             dma((4,)),
             dma((1,)),
@@ -365,17 +471,20 @@
             dma((nc,)),
             dma((nc,)),
             dma((nc,)),
-            dma((nd,)),
-            dma((nd,)),
+            dma((ng, nc)),
+            dma((ng,)),
+            dma((ng, nc)),
+            dma((ng, nc)),
             dma((ng,)),
             dma((ng,)),
-            dma((ng,)),
-            dma((ng,)),
+            dma((2,)),
+            dma((nc,)),
+            dma((nc,)),
             dma((ng,)),
             dma((ng,)),
         ],
         compiler_params=pltpu.CompilerParams(
-            collective_id=0, has_side_effects=True, vmem_limit_bytes=48 * 1024 * 1024
+            collective_id=0, has_side_effects=True, vmem_limit_bytes=63 * 1024 * 1024
         ),
     )(sources, boundary, inverse, flux, leaf_lift, schur, spread, lift)
 

time: 37.7 us -> 29.2 us (0.77)
  local copies, waits for them, and re-layouts: 8.22 us -> 1.67 us
  Pallas kernels: 29.2 us -> 27.3 us
    unnamed x15 -> x1, local copies, waits for them, and re-layouts: 8.22 us -> 1.67 us
    pallas_call x1, Pallas kernels: 29.2 us -> 27.3 us  [body(): pl.pallas_call(functools.partial(kernel, ng, nd, nl), out_shape=jax.Shape...]
where the time goes in v2:
time: 29.2 us; the launch traced here: 28.9 us
  Pallas kernels  27.3 us (93%)
  local copies, waits for them, and re-layouts  1.67 us (6%)
    pallas_call x1, Pallas kernels, body(): pl.pallas_call(functools.partial(kernel, ng, nd, nl), out_shape=jax.Shape...  27.3 us
    unnamed x1, local copies, waits for them, and re-layouts  1.67 us

profile of v2, /device:TPU:0, one launch (start us, length us, event | category | flops | bytes accessed | tf_op | source)
XLA Modules:
  0.0 28.9 jit_solution(16165915777314887707)
XLA Ops:
  0.0 27.3 %shard_map.82 = f32[8,8192]{1,0:T(8,128)} custom-call(bf16[8,4096]{1,0:T(8,128)(2,1)} %src_hbm.1, f32[8,256]{1,0:T(8,128)} %bnd_hbm.1, bf16[4096,2048]{1,0:T(8,128)(2,1)} %inv_hbm.1, bf16[4096,256]{1,0:T(8,128)(2,1)} %flux_hbm.1, bf16[512,2048]{1,0:T(8,128)(2,1)} %ll_hbm.1, f32[4,64,128]{2,1,0:T(8,128)} %schur_hbm.1, f32[4,64,256]{2,1,0:T(8,128)} %spread_hbm.1, ...), custom_call_target="tpu_custom_call" | custom-call | tf_op jit(solution)/shard_map/pallas_call | solution.py:443
  27.3 1.7 %copy.10 = f32[8,8192]{1,0:T(8,128)} copy(f32[8,8192]{1,0:T(8,128)} %shard_map.82) | data formatting | bytes 524288

commit v3 on v2

--- a/solution.py
+++ b/solution.py
@@ -154,82 +154,6 @@
                 barrier, inc=1, device_id=(lax.rem(grp + k, ng), 0), device_id_type=MESH
             )
 
-    @pl.when(dev == 0)
-    def _():
-        pl.semaphore_wait(barrier, nd - 1 + (ng - 1) * npc)
-
-    @pl.when(dev != 0)
-    def _():
-        pl.semaphore_wait(barrier, nd - 1 + ng - 1)
-
-    def remote(src, dst, ssem, rsem, g, d):
-        return pltpu.make_async_remote_copy(
-            src_ref=src, dst_ref=dst, send_sem=ssem, recv_sem=rsem,
-            device_id=(g, d), device_id_type=MESH,
-        )
-
-    def same(ref, ssem, rsem, g, d):
-        return remote(ref, ref, ssem, rsem, g, d)
-
-    fac_send = [
-        same(
-            fac_all.at[dev], fs_sem.at[k], fr_sem.at[k], grp, lax.rem(chip + k, nc) * 2 + core
-        )
-        for k in range(1, nc)
-    ]
-    fac_pass = [
-        same(
-            fac_all.at[lax.rem(chip + nc - k, nc) * 2 + (core if k == 0 else 0)],
-            bs_sem.at[k], br_sem.at[k], grp, sib,
-        )
-        for k in range(nc)
-    ]
-    deal = [
-        remote(
-            fac_all.at[0, pl.ds(c * piece, piece)], top.at[grp, pl.ds(c * piece, piece)],
-            zs_sem.at[k, c], zr_sem.at[k], lax.rem(grp + k, ng), 2 * c,
-        )
-        for k in range(1, ng)
-        for c in range(npc)
-    ]
-    mine = pl.ds(pl.multiple_of(chip * piece, 8), piece)
-
-    def other(k):
-        return lax.rem(grp + ng - k, ng)
-
-    deal_in = [
-        same(top.at[other(k), mine], zs_sem.at[k, 0], zr_sem.at[k], grp, sib)
-        for k in range(1, ng)
-    ]
-    spread_out = [
-        [
-            same(
-                top.at[other(k), mine], hs_sem.at[k, j], hr_sem.at[k, j],
-                grp, lax.rem(chip + j, nc) * 2,
-            )
-            for j in range(1, nc)
-        ]
-        for k in range(1, ng)
-    ]
-    top_pass = [
-        same(top.at[other(k)], ws_sem.at[k], wr_sem.at[k], grp, sib) for k in range(1, ng)
-    ]
-
-    for cp in fa_cp:
-        cp.wait()
-
-    fac_pass[0].start()
-
-    @pl.when(core == 0)
-    def _():
-        for cp in fac_send:
-            cp.start()
-
-    @pl.when(dev == 0)
-    def _():
-        for cp in deal:
-            cp.start()
-
     units = 2 * nl
     rows_u = cells // 2
     inv_cp = [
@@ -279,6 +203,82 @@
         for cp in cps:
             cp.wait()
     pair[core] = climb(outs, lambda s: fac_loc.at[s], lambda s: jump_loc.at[s])
+    @pl.when(dev == 0)
+    def _():
+        pl.semaphore_wait(barrier, nd - 1 + (ng - 1) * npc)
+
+    @pl.when(dev != 0)
+    def _():
+        pl.semaphore_wait(barrier, nd - 1 + ng - 1)
+
+    def remote(src, dst, ssem, rsem, g, d):
+        return pltpu.make_async_remote_copy(
+            src_ref=src, dst_ref=dst, send_sem=ssem, recv_sem=rsem,
+            device_id=(g, d), device_id_type=MESH,
+        )
+
+    def same(ref, ssem, rsem, g, d):
+        return remote(ref, ref, ssem, rsem, g, d)
+
+    fac_send = [
+        same(
+            fac_all.at[dev], fs_sem.at[k], fr_sem.at[k], grp, lax.rem(chip + k, nc) * 2 + core
+        )
+        for k in range(1, nc)
+    ]
+    fac_pass = [
+        same(
+            fac_all.at[lax.rem(chip + nc - k, nc) * 2 + (core if k == 0 else 0)],
+            bs_sem.at[k], br_sem.at[k], grp, sib,
+        )
+        for k in range(nc)
+    ]
+    deal = [
+        remote(
+            fac_all.at[0, pl.ds(c * piece, piece)], top.at[grp, pl.ds(c * piece, piece)],
+            zs_sem.at[k, c], zr_sem.at[k], lax.rem(grp + k, ng), 2 * c,
+        )
+        for k in range(1, ng)
+        for c in range(npc)
+    ]
+    mine = pl.ds(pl.multiple_of(chip * piece, 8), piece)
+
+    def other(k):
+        return lax.rem(grp + ng - k, ng)
+
+    deal_in = [
+        same(top.at[other(k), mine], zs_sem.at[k, 0], zr_sem.at[k], grp, sib)
+        for k in range(1, ng)
+    ]
+    spread_out = [
+        [
+            same(
+                top.at[other(k), mine], hs_sem.at[k, j], hr_sem.at[k, j],
+                grp, lax.rem(chip + j, nc) * 2,
+            )
+            for j in range(1, nc)
+        ]
+        for k in range(1, ng)
+    ]
+    top_pass = [
+        same(top.at[other(k)], ws_sem.at[k], wr_sem.at[k], grp, sib) for k in range(1, ng)
+    ]
+
+    for cp in fa_cp:
+        cp.wait()
+
+    fac_pass[0].start()
+
+    @pl.when(core == 0)
+    def _():
+        for cp in fac_send:
+            cp.start()
+
+    @pl.when(jnp.logical_and(dev == 0, grp > 0))
+    def _():
+        for cp in deal:
+            cp.start()
+
     pair_send = same(pair.at[core], ps_sem.at[0], ps_sem.at[1], grp, sib)
     pair_send.start()
 
@@ -322,9 +322,12 @@
     @pl.when(relay)
     def _():
         for k in range(1, ng):
-            deal_in[k - 1].wait_recv()
-            for cp in spread_out[k - 1]:
-                cp.start()
+
+            @pl.when(other(k) > 0)
+            def _(k=k):
+                deal_in[k - 1].wait_recv()
+                for cp in spread_out[k - 1]:
+                    cp.start()
 
     run_units(cut[1], cut[2])
 
@@ -357,11 +360,8 @@
                 def got(k=k, j=j):
                     spread_out[k - 1][j - 1].wait_recv()
 
-                if npc == nc:
-                    got()
-                else:
-                    pl.when(from_chip < npc)(got)
-            top_pass[k - 1].start()
+                pl.when(jnp.logical_and(from_chip < npc, other(k) > 0))(got)
+            pl.when(other(k) > 0)(top_pass[k - 1].start)
 
     run_units(cut[3], cut[4])
     for cp in groot_send:
@@ -370,8 +370,8 @@
 
     @pl.when(core == 1)
     def _():
-        for cp in top_pass:
-            cp.wait_recv()
+        for k in range(1, ng):
+            pl.when(other(k) > 0)(top_pass[k - 1].wait_recv)
 
     climb([groots[g] for g in range(ng)], lambda s: top.at[s], lambda s: jump_top.at[s])
 
@@ -416,16 +416,21 @@
 
     @pl.when(core == 0)
     def _():
-        for cp in fac_send + fac_pass[1:] + top_pass:
+        for cp in fac_send + fac_pass[1:]:
             cp.wait_send()
+        for k in range(1, ng):
+            pl.when(other(k) > 0)(top_pass[k - 1].wait_send)
 
     @pl.when(relay)
     def _():
-        for cps in spread_out:
-            for cp in cps:
-                cp.wait_send()
-
-    @pl.when(dev == 0)
+        for k in range(1, ng):
+
+            @pl.when(other(k) > 0)
+            def _(k=k):
+                for cp in spread_out[k - 1]:
+                    cp.wait_send()
+
+    @pl.when(jnp.logical_and(dev == 0, grp > 0))
     def _():
         for cp in deal:
             cp.wait_send()

time: 29.2 us -> 29.3 us (level)
  no operation moved by 1% of the time
where the time goes in v3:
time: 29.3 us; the launch traced here: 29 us
  Pallas kernels  27.3 us (93%)
  local copies, waits for them, and re-layouts  1.67 us (6%)
    pallas_call x1, Pallas kernels, body(): pl.pallas_call(functools.partial(kernel, ng, nd, nl), out_shape=jax.Shape...  27.3 us
    unnamed x1, local copies, waits for them, and re-layouts  1.67 us

profile of v3, /device:TPU:0, one launch (start us, length us, event | category | flops | bytes accessed | tf_op | source)
XLA Modules:
  0.0 29.0 jit_solution(2317598244551007281)
XLA Ops:
  0.0 27.3 %shard_map.82 = f32[8,8192]{1,0:T(8,128)} custom-call(bf16[8,4096]{1,0:T(8,128)(2,1)} %src_hbm.1, f32[8,256]{1,0:T(8,128)} %bnd_hbm.1, bf16[4096,2048]{1,0:T(8,128)(2,1)} %inv_hbm.1, bf16[4096,256]{1,0:T(8,128)(2,1)} %flux_hbm.1, bf16[512,2048]{1,0:T(8,128)(2,1)} %ll_hbm.1, f32[4,64,128]{2,1,0:T(8,128)} %schur_hbm.1, f32[4,64,256]{2,1,0:T(8,128)} %spread_hbm.1, ...), custom_call_target="tpu_custom_call" | custom-call | tf_op jit(solution)/shard_map/pallas_call | solution.py:448
  27.3 1.7 %copy.10 = f32[8,8192]{1,0:T(8,128)} copy(f32[8,8192]{1,0:T(8,128)} %shard_map.82) | data formatting | bytes 524288
